TPU v7x, 512 devices: a whole 4x4x16 slice. The times are simulated.
512 devices in a mesh: gx: 16 (over y, z_hi, core), gy: 32 (over x, z_lo).
Axes of the slice: x: 4, y: 4, z: 16 (z_hi: 2, z_lo: 8; z = z_hi * 8 + z_lo), core: 2. Of those that a mesh axis runs over, the one named last changes fastest.
Arguments:
- tokens: bfloat16 [512, 16384], P('gy', 'gx'), may hold values from -6 to 6
- gate_weight: bfloat16 [16384, 26624], P('gx', 'gy'), may hold values from -0.046875 to 0.046875
- up_weight: bfloat16 [16384, 26624], P('gx', 'gy'), may hold values from -0.046875 to 0.046875
- down_weight: bfloat16 [26624, 16384], P('gy', 'gx'), may hold values from -0.0390625 to 0.0390625
Outputs:
- mixed: bfloat16 [512, 16384], P('gy', 'gx')
All inputs are finite; a program needn't handle non-finite values.
Results may differ from a plain program's by a relative error of at most 0.0049.
Values may be sent and summed in bfloat16 or wider, within the bound.
No kernel may reach another device: no remote copies, remote signals or barrier semaphores. Data moves between devices by JAX's collectives and lax.ppermute only.
A program may use at most 64 MiB of HBM per device.

v0:
```python
import jax
import jax.numpy as jnp
from jax import lax
from jax.sharding import PartitionSpec as P


def on_device(tokens, gate_weight, up_weight, down_weight):
    piece = lax.all_gather(tokens, "gy", axis=0, tiled=True)
    gate_part = jnp.dot(piece, gate_weight, preferred_element_type=jnp.float32)
    up_part = jnp.dot(piece, up_weight, preferred_element_type=jnp.float32)
    partial_value = jnp.stack([gate_part, up_part])
    summed = lax.psum(partial_value, "gx")
    hidden = (jax.nn.silu(summed[0]) * summed[1]).astype(jnp.bfloat16)
    mixed = lax.psum_scatter(
        jnp.dot(hidden, down_weight, preferred_element_type=jnp.float32),
        "gy",
        scatter_dimension=0,
        tiled=True,
    )
    return mixed.astype(jnp.bfloat16)


def solution(mesh):
    return jax.shard_map(
        on_device,
        mesh=mesh,
        in_specs=(P("gy", "gx"), P("gx", "gy"), P("gx", "gy"), P("gy", "gx")),
        out_specs=P("gy", "gx"),
        check_vma=False,
    )
```

profile of v0, /device:TPU:16, one launch (start us, length us, event | category | flops | bytes accessed | tf_op | source)
XLA Modules:
  0.0 865.9 jit_solution(11074020991371853969)
XLA Ops:
  6.5 0.0 copy-start
  6.5 0.0 all-gather.2.cloned.1.call-start
  6.5 0.7 all-gather.2.cloned.1.call-update
  7.3 0.0 copy-start.1
  7.3 0.0 all-reduce.2.cloned.1.call-start
  7.3 228.6 %all-gather.2.cloned.1.call-done = bf16[512,1024]{1,0:T(8,128)(2,1)} async-done(((bf16[16,1024]{1,0:T(8,128)(2,1)}), bf16[512,1024]{1,0:T(8,128)(2,1)}) %all-gather.2.cloned.1.call-update) | async-done | bytes 1048592 | tf_op jit(solution)/shard_map/all_gather | solution.py:8
  235.9 0.0 copy-start.2
  235.9 2.9 convolution_bitcast_fusion
  238.9 0.0 copy-done.1
  238.9 0.0 copy-done.2
  238.9 1.1 convolution_bitcast_fusion.1
  240.0 2.1 pad_maximum_fusion
  242.1 0.0 all-reduce.2.cloned.1.call-update
  242.1 0.0 reduce-scatter.2.cloned.1.call-start
  242.2 363.3 %all-reduce.2.cloned.1.call-done = f32[2,512,832]{1,2,0:T(8,128)} async-done(((f32[2,512,832]{1,2,0:T(8,128)}), f32[2,512,832]{1,2,0:T(8,128)}) %all-reduce.2.cloned.1.call-update) | async-done | bytes 3407888 | tf_op jit(solution)/shard_map/psum | solution.py:12
  605.5 0.0 copy-done
  605.5 4.7 fusion.2
  610.2 0.0 reduce-scatter.2.cloned.1.call-update
  610.2 247.7 %reduce-scatter.2.cloned.1.call-done = f32[16,1024]{1,0:T(8,128)} async-done(((f32[512,1024]{1,0:T(8,128)}), f32[16,1024]{1,0:T(8,128)}) %reduce-scatter.2.cloned.1.call-update) | async-done | bytes 65552 | tf_op jit(solution)/shard_map/reduce_scatter | solution.py:14
  857.9 1.5 convert_element_type.7
Async XLA Ops:
  6.5 599.0 %copy-start = (bf16[832,1024]{1,0:T(8,128)(2,1)S(1)}, bf16[832,1024]{1,0:T(8,128)(2,1)}, u32[]{:S(2)}) copy-start(bf16[832,1024]{1,0:T(8,128)(2,1)} %param.7) | copy-start | bytes 5111812
  6.5 229.4 %all-gather.2.cloned.1.call-start = ((), (), s32[]{:S(2)}) async-start(), calls=%async_computation.1 | async-start | bytes 1081344 | tf_op jit(solution)/shard_map/all_gather | solution.py:8
  7.3 231.6 %copy-start.1 = (bf16[1024,832]{0,1:T(8,128)(2,1)S(1)}, bf16[1024,832]{0,1:T(8,128)(2,1)}, u32[]{:S(2)}) copy-start(bf16[1024,832]{0,1:T(8,128)(2,1)} %param.5) | copy-start | bytes 5111812
  7.3 598.2 %all-reduce.2.cloned.1.call-start = ((), (), s32[]{:S(2)}) async-start(), calls=%async_computation.2 | async-start | bytes 6815744 | tf_op jit(solution)/shard_map/psum | solution.py:12
  235.9 3.0 copy-start.2
  242.1 615.7 %reduce-scatter.2.cloned.1.call-start = ((), (), s32[]{:S(2)}) async-start(), calls=%async_computation.3 | async-start | bytes 2162688 | tf_op jit(solution)/shard_map/reduce_scatter | solution.py:14
Sparse Core Ops, SparseCore 0:
  9.4 226.4 all-gather.1
  242.3 363.1 all-reduce.1
  610.3 247.5 reduce-scatter.1
where the time goes:
time: 866 us
  waiting for transfers between devices  840 us (97%)
  between operations  13.1 us (2%)
  matrix products  8.7 us (1%)
    psum x1, waiting for transfers between devices, on_device(): summed = lax.psum(partial_value, 'gx')  363 us
    reduce_scatter x1, waiting for transfers between devices, on_device(): lax.psum_scatter(jnp.dot(hidden, down_weight, preferred_element_type=jnp....  248 us
    all_gather x1, waiting for transfers between devices, on_device(): piece = lax.all_gather(tokens, 'gy', axis=0, tiled=True)  229 us
  transfers between devices with their start and end apart: 3, of which 3 were waited for; matrix products, arithmetic and copies ran while one was open for 0% of the time, Pallas kernels for 0%

commit v1 on v0

--- a/solution.py
+++ b/solution.py
@@ -5,7 +5,10 @@
 
 
 def on_device(tokens, gate_weight, up_weight, down_weight):
-    piece = lax.all_gather(tokens, "gy", axis=0, tiled=True)
+    devices = lax.axis_size("gy")
+    blocks = jnp.stack([tokens for _ in range(devices)])
+    blocks = lax.all_to_all(blocks, "gy", split_axis=0, concat_axis=0)
+    piece = jnp.concatenate(blocks, axis=0)
     gate_part = jnp.dot(piece, gate_weight, preferred_element_type=jnp.float32)
     up_part = jnp.dot(piece, up_weight, preferred_element_type=jnp.float32)
     partial_value = jnp.stack([gate_part, up_part])

time: 866 us -> 702 us (0.81)
  the two profiles are of different devices: /device:TPU:16 before, /device:TPU:8 now
where the time goes in v1:
time: 702 us
  waiting for transfers between devices  610 us (87%)
  blocking collectives  66.4 us (9%)
  between operations  13.4 us (2%)
    psum x1, waiting for transfers between devices, on_device(): summed = lax.psum(partial_value, 'gx')  369 us
    reduce_scatter x1, waiting for transfers between devices, on_device(): lax.psum_scatter(jnp.dot(hidden, down_weight, preferred_element_type=jnp....  242 us
    all_to_all x1, blocking collectives, on_device(): blocks = lax.all_to_all(blocks, 'gy', split_axis=0, concat_axis=0)  66.4 us
  transfers between devices with their start and end apart: 2, of which 2 were waited for; matrix products, arithmetic and copies ran while one was open for 0% of the time, Pallas kernels for 0%

profile of v1, /device:TPU:8, one launch (start us, length us, event | category | flops | bytes accessed | tf_op | source)
XLA Modules:
  0.0 702.0 jit_solution(4646711859678384553)
XLA Ops:
  6.5 0.0 copy-start
  6.5 0.0 copy-start.1
  6.5 0.0 all-reduce.2.cloned.1.call-start
  6.5 1.0 stack.8
  7.6 66.4 %all_to_all.5 = bf16[32,16,1024]{2,1,0:T(8,128)(2,1)S(1)} all-to-all(bf16[32,16,1024]{2,1,0:T(8,128)(2,1)S(1)} %stack.8), channel_id=1, replica_groups=mesh['gx'=16,'gy'=32] {'gy'}, dimensions={0} | all-to-all | bytes 2097152 | tf_op jit(solution)/shard_map/all_to_all | solution.py:10
  73.9 0.0 copy-done.1
  73.9 0.0 copy-start.2
  73.9 1.1 convolution_bitcast_fusion
  75.0 0.4 copy-done.2
  75.4 1.1 convolution_bitcast_fusion.1
  76.5 2.1 pad_maximum_fusion
  78.6 0.0 all-reduce.2.cloned.1.call-update
  78.6 0.0 reduce-scatter.2.cloned.1.call-start
  78.7 368.7 %all-reduce.2.cloned.1.call-done = f32[2,512,832]{1,2,0:T(8,128)} async-done(((f32[2,512,832]{1,2,0:T(8,128)}), f32[2,512,832]{1,2,0:T(8,128)}) %all-reduce.2.cloned.1.call-update) | async-done | bytes 3407888 | tf_op jit(solution)/shard_map/psum | solution.py:15
  447.3 0.0 copy-done
  447.3 4.7 fusion.2
  452.0 0.0 reduce-scatter.2.cloned.1.call-update
  452.0 241.6 %reduce-scatter.2.cloned.1.call-done = f32[16,1024]{1,0:T(8,128)} async-done(((f32[512,1024]{1,0:T(8,128)}), f32[16,1024]{1,0:T(8,128)}) %reduce-scatter.2.cloned.1.call-update) | async-done | bytes 65552 | tf_op jit(solution)/shard_map/reduce_scatter | solution.py:17
  693.7 1.5 convert_element_type.7
Async XLA Ops:
  6.5 440.8 %copy-start = (bf16[832,1024]{1,0:T(8,128)(2,1)S(1)}, bf16[832,1024]{1,0:T(8,128)(2,1)}, u32[]{:S(2)}) copy-start(bf16[832,1024]{1,0:T(8,128)(2,1)} %param.7) | copy-start | bytes 5111812
  6.5 67.4 %copy-start.1 = (bf16[1024,832]{0,1:T(8,128)(2,1)S(1)}, bf16[1024,832]{0,1:T(8,128)(2,1)}, u32[]{:S(2)}) copy-start(bf16[1024,832]{0,1:T(8,128)(2,1)} %param.6) | copy-start | bytes 5111812
  6.5 440.8 %all-reduce.2.cloned.1.call-start = ((), (), s32[]{:S(2)}) async-start(), calls=%async_computation.2 | async-start | bytes 6815744 | tf_op jit(solution)/shard_map/psum | solution.py:15
  73.9 1.5 copy-start.2
  78.6 615.0 %reduce-scatter.2.cloned.1.call-start = ((), (), s32[]{:S(2)}) async-start(), calls=%async_computation.3 | async-start | bytes 2162688 | tf_op jit(solution)/shard_map/reduce_scatter | solution.py:17
Sparse Core Ops, SparseCore 0:
  78.7 368.5 all-reduce.1
  452.2 241.4 reduce-scatter.1
